TPU v7x, 512 devices: a whole 4x8x8 slice. The times are simulated.
512 devices in a mesh: dp: 2 (over core), ctx: 64 (over z, y), head: 4 (over x).
Axes of the slice: x: 4, y: 8, z: 8, core: 2. Of those that a mesh axis runs over, the one named last changes fastest.
Arguments:
- queries: bfloat16 [2, 8192, 2560], P('dp', 'ctx', 'head'), may hold values from -25 to 25
- keys: bfloat16 [2, 8192, 2560], P('dp', 'ctx', 'head'), may hold values from -25 to 25
- values: bfloat16 [2, 8192, 2560], P('dp', 'ctx', 'head'), may hold values from -6 to 6
- grad_y: bfloat16 [2, 8192, 2560], P('dp', 'ctx', 'head'), may hold values from -6 to 6
- out_gain: float32 [2560], P('head'), may hold values from 0.1 to 1.9
- offsets: int32 [2, 20], P(None, 'head'), may hold values from 0 to 63, as said below
Outputs:
- attended: bfloat16 [2, 8192, 2560], P('dp', 'ctx', 'head')
- query_grad: bfloat16 [2, 8192, 2560], P('dp', 'ctx', 'head')
- key_grad: bfloat16 [2, 8192, 2560], P('dp', 'ctx', 'head')
- value_grad: bfloat16 [2, 8192, 2560], P('dp', 'ctx', 'head')
- gain_grad: float32 [2560], P('head')
Inputs may be any that keep to these rules, and one draw needn't show every extreme that they name: Row 0 holds offsets below 8, row 1 offsets below 64.
All inputs are finite; a program needn't handle non-finite values.
Results may differ from a plain program's by a relative error of at most 0.011.
Values may be sent and summed in bfloat16 or wider, within the bound.
A program may use at most 64 MiB of HBM per device.

v0:
```python
import math
import jax
import jax.numpy as jnp
from jax import lax
from jax.sharding import PartitionSpec as P

HEAD_DIM = 128
SPAN = 4
R1 = 8
EPS = 1e-06


def swapped(block, axis, bit):
    count = lax.axis_size(axis)
    route = []
    for low in range(count):
        high = low | 1 << bit
        if high != low and high < count:
            route += [(low, high), (high, low)]
    return lax.ppermute(block, axis, route)


def pick_rows(source_rows, dilation, shifts):
    row_count, head_count, head_width = source_rows.shape
    grouped = source_rows.reshape(row_count // dilation, dilation, head_count, head_width)
    hit_mask = jnp.arange(dilation, dtype=jnp.int32).reshape(1, dilation, 1, 1) == shifts.reshape(
        1, 1, head_count, 1
    )
    chosen = jnp.where(hit_mask, grouped, jnp.zeros((), source_rows.dtype))
    return jnp.sum(chosen, axis=1, dtype=source_rows.dtype)


def place_rows(row_values, dilation, shifts):
    row_count, head_count, head_width = row_values.shape
    hit_mask = jnp.arange(dilation, dtype=jnp.int32).reshape(1, dilation, 1, 1) == shifts.reshape(
        1, 1, head_count, 1
    )
    spread = jnp.where(hit_mask, row_values[:, None], jnp.zeros((), row_values.dtype))
    return spread.reshape(row_count * dilation, head_count, head_width)


def level_scores(q_rows, k_rows):
    score_scale = 1.0 / math.sqrt(q_rows.shape[-1])
    return (
        jnp.einsum("qhe,khe->hqk", q_rows, k_rows, preferred_element_type=jnp.float32) * score_scale
    )


def attend(q_rows, k_rows, v_rows):
    scores = level_scores(q_rows, k_rows)
    row_max = jnp.max(scores, axis=-1, keepdims=True)
    log_total = row_max[..., 0] + jnp.log(jnp.sum(jnp.exp(scores - row_max), axis=-1))
    soft_rows = jnp.exp(scores - log_total[..., None]).astype(jnp.bfloat16)
    level_out = jnp.einsum("hqk,khe->qhe", soft_rows, v_rows, preferred_element_type=jnp.float32)
    return (level_out, log_total.T)


def score_grads(q_rows, k_rows, v_rows, log_total, grad_low, row_shift):
    score_scale = 1.0 / math.sqrt(q_rows.shape[-1])
    scores = level_scores(q_rows, k_rows)
    exact_soft = jnp.exp(scores - log_total.T[..., None])
    prob_grad = jnp.einsum("qhe,khe->hqk", grad_low, v_rows, preferred_element_type=jnp.float32)
    score_grad = (exact_soft * (prob_grad + row_shift.T[..., None]) * score_scale).astype(
        jnp.bfloat16
    )
    return (score_grad, exact_soft.astype(jnp.bfloat16))


def key_parts(score_grad, soft_low, q_rows, grad_low):
    k_part = jnp.einsum("hqk,qhe->khe", score_grad, q_rows, preferred_element_type=jnp.float32)
    v_part = jnp.einsum("hqk,qhe->khe", soft_low, grad_low, preferred_element_type=jnp.float32)
    return (k_part, v_part)


def query_part(score_grad, k_rows):
    return jnp.einsum("hqk,khe->qhe", score_grad, k_rows, preferred_element_type=jnp.float32)


def shards(queries, keys, values, grad_y, out_gain, offsets):
    tokens = queries.shape[1]
    flat_width = queries.shape[2]
    head_count = flat_width // HEAD_DIM
    row_shape = (tokens, head_count, HEAD_DIM)
    q_own = queries[0].reshape(row_shape)
    k_own = keys[0].reshape(row_shape)
    v_own = values[0].reshape(row_shape)
    ctx_size = lax.axis_size("ctx")
    span_bits = SPAN.bit_length() - 1
    my_place = lax.axis_index("ctx")
    mid_shift = offsets[0]
    top_shift = offsets[1]
    positions = jnp.arange(tokens, dtype=jnp.int32)
    mid_hit = (positions % R1)[:, None] == mid_shift[None, :]
    top_hit = (positions % ctx_size)[:, None] == top_shift[None, :]
    mid_q = pick_rows(q_own, R1, mid_shift)
    mid_k = pick_rows(k_own, R1, mid_shift)
    mid_v = pick_rows(v_own, R1, mid_shift)
    top_q = pick_rows(q_own, ctx_size, top_shift)
    top_k = pick_rows(k_own, ctx_size, top_shift)
    top_v = pick_rows(v_own, ctx_size, top_shift)
    mid_keys = mid_k.reshape(-1, flat_width)
    mid_vals = mid_v.reshape(-1, flat_width)
    top_keys = top_k.reshape(-1, flat_width)
    top_vals = top_v.reshape(-1, flat_width)

    def append_peer(mine, received, level_bit):
        upper_side = my_place >> level_bit & 1 == 1
        return jnp.where(
            upper_side, jnp.concatenate([received, mine], 0), jnp.concatenate([mine, received], 0)
        )

    for level_bit in range(span_bits):
        received = swapped((mid_keys, mid_vals), "ctx", level_bit)
        mid_keys = append_peer(mid_keys, received[0], level_bit)
        mid_vals = append_peer(mid_vals, received[1], level_bit)
    top_keys, top_vals = (
        lax.all_gather(top_keys, "ctx", axis=0, tiled=True),
        lax.all_gather(top_vals, "ctx", axis=0, tiled=True),
    )
    mid_keys = mid_keys.reshape(-1, head_count, HEAD_DIM)
    mid_vals = mid_vals.reshape(-1, head_count, HEAD_DIM)
    top_keys = top_keys.reshape(-1, head_count, HEAD_DIM)
    top_vals = top_vals.reshape(-1, head_count, HEAD_DIM)
    base_out, base_total = attend(q_own, k_own, v_own)
    mid_out, mid_total = attend(mid_q, mid_keys, mid_vals)
    top_out, top_total = attend(top_q, top_keys, top_vals)
    mid_full = place_rows(mid_total[..., None], R1, mid_shift)[..., 0]
    top_full = place_rows(top_total[..., None], ctx_size, top_shift)[..., 0]
    row_max = jnp.maximum(base_total, jnp.where(mid_hit, mid_full, base_total))
    row_max = jnp.maximum(row_max, jnp.where(top_hit, top_full, base_total))
    base_expo = jnp.exp(base_total - row_max)
    mid_expo = jnp.where(mid_hit, jnp.exp(mid_full - row_max), 0.0)
    top_expo = jnp.where(top_hit, jnp.exp(top_full - row_max), 0.0)
    denom = base_expo + mid_expo + top_expo
    base_share = base_expo / denom
    mid_share = mid_expo / denom
    top_share = top_expo / denom
    attn = (
        base_share[..., None] * base_out
        + mid_share[..., None] * place_rows(mid_out, R1, mid_shift)
        + top_share[..., None] * place_rows(top_out, ctx_size, top_shift)
    )
    inv_rms = lax.rsqrt(jnp.mean(attn * attn, axis=-1, keepdims=True) + EPS)
    normed = attn * inv_rms
    gain_rows = out_gain.reshape(head_count, HEAD_DIM)
    attended = (normed * gain_rows).astype(jnp.bfloat16).reshape(1, tokens, flat_width)
    grad_full = grad_y[0].reshape(row_shape).astype(jnp.float32)
    gain_part = jnp.sum(grad_full * normed, axis=0).reshape(flat_width)
    gain_grad = lax.psum(gain_part, ("dp", "ctx"))
    grad_norm = grad_full * gain_rows
    grad_attn = inv_rms * (
        grad_norm - normed * jnp.mean(grad_norm * normed, axis=-1, keepdims=True)
    )
    inner = jnp.sum(grad_attn * attn, axis=-1)
    base_low = (base_share[..., None] * grad_attn).astype(jnp.bfloat16)
    base_shift = -(base_share * inner)
    base_grad, base_soft = score_grads(q_own, k_own, v_own, base_total, base_low, base_shift)
    base_dq = query_part(base_grad, k_own)
    base_dk, base_dv = key_parts(base_grad, base_soft, q_own, base_low)
    mid_sel = pick_rows(mid_share[..., None], R1, mid_shift)[..., 0]
    mid_low = (mid_sel[..., None] * pick_rows(grad_attn, R1, mid_shift)).astype(jnp.bfloat16)
    mid_row_shift = -(mid_sel * pick_rows(inner[..., None], R1, mid_shift)[..., 0])
    mid_grad, mid_soft = score_grads(mid_q, mid_keys, mid_vals, mid_total, mid_low, mid_row_shift)
    mid_dq = query_part(mid_grad, mid_keys)
    mid_dk, mid_dv = key_parts(mid_grad, mid_soft, mid_q, mid_low)
    mid_dk = mid_dk.reshape(-1, flat_width)
    mid_dv = mid_dv.reshape(-1, flat_width)
    for level_bit in reversed(range(span_bits)):
        half_rows = mid_dk.shape[0] // 2
        upper_side = my_place >> level_bit & 1 == 1
        keep_k = jnp.where(upper_side, mid_dk[half_rows:], mid_dk[:half_rows])
        keep_v = jnp.where(upper_side, mid_dv[half_rows:], mid_dv[:half_rows])
        send_k = jnp.where(upper_side, mid_dk[:half_rows], mid_dk[half_rows:])
        send_v = jnp.where(upper_side, mid_dv[:half_rows], mid_dv[half_rows:])
        received = (
            swapped(send_k.astype(jnp.bfloat16), "ctx", level_bit).astype(send_k.dtype),
            swapped(send_v.astype(jnp.bfloat16), "ctx", level_bit).astype(send_v.dtype),
        )
        mid_dk = keep_k + received[0]
        mid_dv = keep_v + received[1]
    mid_dk = mid_dk.reshape(-1, head_count, HEAD_DIM)
    mid_dv = mid_dv.reshape(-1, head_count, HEAD_DIM)
    top_sel = pick_rows(top_share[..., None], ctx_size, top_shift)[..., 0]
    top_low = (top_sel[..., None] * pick_rows(grad_attn, ctx_size, top_shift)).astype(jnp.bfloat16)
    top_row_shift = -(top_sel * pick_rows(inner[..., None], ctx_size, top_shift)[..., 0])
    top_grad, top_soft = score_grads(top_q, top_keys, top_vals, top_total, top_low, top_row_shift)
    top_dq = query_part(top_grad, top_keys)
    gathered_dk, gathered_dv = key_parts(top_grad, top_soft, top_q, top_low)
    summed = (
        lax.psum_scatter(
            gathered_dk.reshape(-1, flat_width), "ctx", scatter_dimension=0, tiled=True
        ),
        lax.psum_scatter(
            gathered_dv.reshape(-1, flat_width), "ctx", scatter_dimension=0, tiled=True
        ),
    )
    top_dk = summed[0].reshape(-1, head_count, HEAD_DIM)
    top_dv = summed[1].reshape(-1, head_count, HEAD_DIM)
    query_grad = (
        base_dq + place_rows(mid_dq, R1, mid_shift) + place_rows(top_dq, ctx_size, top_shift)
    )
    key_grad = base_dk + place_rows(mid_dk, R1, mid_shift) + place_rows(top_dk, ctx_size, top_shift)
    value_grad = (
        base_dv + place_rows(mid_dv, R1, mid_shift) + place_rows(top_dv, ctx_size, top_shift)
    )
    out_shape = (1, tokens, flat_width)
    return (
        attended,
        query_grad.astype(jnp.bfloat16).reshape(out_shape),
        key_grad.astype(jnp.bfloat16).reshape(out_shape),
        value_grad.astype(jnp.bfloat16).reshape(out_shape),
        gain_grad,
    )


def solution(mesh):
    in_specs = (
        P("dp", "ctx", "head"),
        P("dp", "ctx", "head"),
        P("dp", "ctx", "head"),
        P("dp", "ctx", "head"),
        P("head"),
        P(None, "head"),
    )
    out_specs = (
        P("dp", "ctx", "head"),
        P("dp", "ctx", "head"),
        P("dp", "ctx", "head"),
        P("dp", "ctx", "head"),
        P("head"),
    )
    return jax.shard_map(shards, mesh=mesh, in_specs=in_specs, out_specs=out_specs, check_vma=False)
```

profile of v0, /device:TPU:266, one launch (start us, length us, event | category | flops | bytes accessed | tf_op | source)
XLA Modules:
  0.0 443.0 jit_solution(7934693849912801585)
XLA Ops:
  7.2 0.8 slice_bitcast_fusion.1
  8.0 1.5 fusion.26
  9.6 2.4 collective-permute-start
  12.0 3.6 collective-permute-start.2
  15.6 0.2 copy.143
  15.8 0.2 copy.144
  15.9 0.2 reshape_reshape_squeeze.20
  16.2 0.2 reshape_reshape_squeeze.21
  16.4 0.7 copy-done.2
  17.1 0.2 reshape_reshape_squeeze.23
  17.5 0.3 select_reduce_fusion
  17.8 48.5 %all-gather = bf16[64,2,640]{2,1,0:T(2,128)(2,1)S(1)} all-gather(bf16[1,2,640]{2,1,0:T(2,128)(2,1)S(1)} %reshape.367), channel_id=1, replica_groups=mesh['dp'=2,'ctx'=64,'head'=4] {'ctx'}, dimensions={0}, use_global_device_ids=true | all-gather | bytes 166400 | tf_op jit(solution)/shard_map/all_gather | solution.py:117
  66.4 0.3 fusion.58
  66.7 0.2 exponential_reduce_fusion.2
  67.0 47.4 %all-gather.1 = bf16[64,2,640]{2,1,0:T(2,128)(2,1)S(1)} all-gather(bf16[1,2,640]{2,1,0:T(2,128)(2,1)S(1)} %reshape.369), channel_id=1, replica_groups=mesh['dp'=2,'ctx'=64,'head'=4] {'ctx'}, dimensions={0}, use_global_device_ids=true | all-gather | bytes 166400 | tf_op jit(solution)/shard_map/all_gather | solution.py:118
  114.4 0.2 convolution_bitcast_fusion.9
  114.6 0.3 fusion.60
  115.0 0.2 copy.157
  115.4 0.5 copy-done.4
  115.9 0.2 copy.168
  116.1 0.2 copy.169
  116.4 1.3 dynamic-slice
  118.4 4.6 %collective-permute-start.1 = (bf16[32,640]{1,0:T(8,128)(2,1)S(1)}, bf16[32,640]{1,0:T(8,128)(2,1)S(1)}, u32[]{:S(2)}, u32[]{:S(2)}) collective-permute-start(bf16[32,640]{1,0:T(8,128)(2,1)S(1)} %maximum_select_fusion.2), channel_id=1, source_target_pairs={{0,8},{8,0},{4,12},{12,4},{16,24},{24,16},{20,28},{28,20},{32,40},... | collective-permute-start | bytes 122888 | tf_op jit(solution)/shard_map/ppermute | solution.py:20
  123.0 2.2 collective-permute-start.3
  125.3 0.2 fusion.59
  125.5 0.2 exponential_reduce_fusion.1
  126.2 0.2 fusion.23
  126.4 3.4 collective-permute-done.3
  129.8 0.2 convolution_bitcast_fusion.7
  130.0 0.5 multiply_reduce_fusion.3
  130.6 0.7 copy-done.5
  131.2 0.3 multiply_reduce_fusion
  131.5 0.3 fusion.22
  131.8 0.2 multiply_reduce_fusion.1
  132.1 0.2 fusion.21
  132.7 0.2 fusion.20
  132.9 0.2 convolution_bitcast_fusion.8
  133.0 1.0 fusion.50
  134.1 1.0 fusion.47
  135.1 0.4 fusion.14
  135.6 0.3 convolution_bitcast_fusion.4
  135.9 0.2 fusion.17
  136.1 2.2 collective-permute-start.6
  138.3 0.2 convolution_bitcast_fusion.5
  138.7 4.6 %collective-permute-start.4 = (bf16[32,640]{1,0:T(8,128)(2,1)S(1)}, bf16[32,640]{1,0:T(8,128)(2,1)S(1)}, u32[]{:S(2)}, u32[]{:S(2)}) collective-permute-start(bf16[32,640]{1,0:T(8,128)(2,1)S(1)} %copy_bitcast_fusion.1), channel_id=1, source_target_pairs={{0,8},{8,0},{4,12},{12,4},{16,24},{24,16},{20,28},{28,20},{32,40},... | collective-permute-start | bytes 122888 | tf_op jit(solution)/shard_map/ppermute | solution.py:20
  143.3 0.2 copy.167
  143.4 0.8 copy.198
  144.3 275.7 %psum.7 = f32[640]{0:T(1024)} all-reduce(f32[640]{0:T(1024)S(1)} %bitcast.253), channel_id=1, replica_groups=mesh['dp'=2,'ctx'=64,'head'=4] {'dp','ctx'}, use_global_device_ids=true, to_apply=%region_24.25 | all-reduce | flops 640 | bytes 5120 | tf_op jit(solution)/shard_map/psum | solution.py:149
  420.0 4.7 %collective-permute-start.7 = (bf16[16,640]{1,0:T(8,128)(2,1)S(1)}, bf16[16,640]{1,0:T(8,128)(2,1)S(1)}, u32[]{:S(2)}, u32[]{:S(2)}) collective-permute-start(bf16[16,640]{1,0:T(8,128)(2,1)S(1)} %select_convert_fusion.2), channel_id=1, source_target_pairs={{0,4},{4,0},{8,12},{12,8},{16,20},{20,16},{24,28},{28,24},{32,36},... | collective-permute-start | bytes 61448 | tf_op jit(solution)/shard_map/ppermute | solution.py:20
  424.8 1.9 collective-permute-start.5
  426.8 3.7 collective-permute-done.5
  430.6 1.2 constant_dynamic-slice_fusion.1
  431.8 0.1 constant_dynamic-slice_fusion
  432.0 0.2 copy.186
  432.2 0.2 bitcast_select_fusion
  432.4 0.2 fusion.12
  432.6 0.2 copy.187
  432.8 0.8 copy.200
  433.6 0.3 fusion.11
  433.9 0.2 copy.179
  434.1 0.8 copy.199
  434.9 0.3 fusion.13
  435.2 0.2 copy.196
  435.4 0.8 copy.201
  (73 shorter events, 2.7 us)
Async XLA Ops:
  7.2 423.4 %all-reduce.5.cloned.1.call-start = ((), (), s32[]{:S(2)}) async-start(), calls=%async_computation | async-start | bytes 1310720
  8.0 7.6 %copy-start = (bf16[1,128,640]{2,1,0:T(8,128)(2,1)S(1)}, bf16[1,128,640]{2,1,0:T(8,128)(2,1)}, u32[]{:S(2)}) copy-start(bf16[1,128,640]{2,1,0:T(8,128)(2,1)} %param.6) | copy-start | bytes 491524
  9.6 108.7 %collective-permute-start = (bf16[16,640]{1,0:T(8,128)(2,1)S(1)}, bf16[16,640]{1,0:T(8,128)(2,1)S(1)}, u32[]{:S(2)}, u32[]{:S(2)}) collective-permute-start(bf16[16,640]{1,0:T(8,128)(2,1)S(1)} %copy_bitcast_fusion.7), channel_id=1, source_target_pairs={{0,4},{4,0},{8,12},{12,8},{16,20},{20,16},{24,28},{28,24},{32,36},... | collective-permute-start | bytes 61448 | tf_op jit(solution)/shard_map/ppermute | solution.py:20
  12.0 3.8 copy-start.1
  12.0 106.4 %collective-permute-start.2 = (bf16[16,640]{1,0:T(8,128)(2,1)S(1)}, bf16[16,640]{1,0:T(8,128)(2,1)S(1)}, u32[]{:S(2)}, u32[]{:S(2)}) collective-permute-start(bf16[16,640]{1,0:T(8,128)(2,1)S(1)} %copy_bitcast_fusion.6), channel_id=1, source_target_pairs={{0,4},{4,0},{8,12},{12,8},{16,20},{20,16},{24,28},{28,24},{32,36},... | collective-permute-start | bytes 61448 | tf_op jit(solution)/shard_map/ppermute | solution.py:20
  16.2 0.9 copy-start.2
  115.0 0.9 copy-start.4
  118.4 6.9 %collective-permute-start.1 = (bf16[32,640]{1,0:T(8,128)(2,1)S(1)}, bf16[32,640]{1,0:T(8,128)(2,1)S(1)}, u32[]{:S(2)}, u32[]{:S(2)}) collective-permute-start(bf16[32,640]{1,0:T(8,128)(2,1)S(1)} %maximum_select_fusion.2), channel_id=1, source_target_pairs={{0,8},{8,0},{4,12},{12,4},{16,24},{24,16},{20,28},{28,20},{32,40},... | collective-permute-start | bytes 122888 | tf_op jit(solution)/shard_map/ppermute | solution.py:20
  123.0 6.8 %collective-permute-start.3 = (bf16[32,640]{1,0:T(8,128)(2,1)S(1)}, bf16[32,640]{1,0:T(8,128)(2,1)S(1)}, u32[]{:S(2)}, u32[]{:S(2)}) collective-permute-start(bf16[32,640]{1,0:T(8,128)(2,1)S(1)} %maximum_select_fusion.4), channel_id=1, source_target_pairs={{0,8},{8,0},{4,12},{12,4},{16,24},{24,16},{20,28},{28,20},{32,40},... | collective-permute-start | bytes 122888 | tf_op jit(solution)/shard_map/ppermute | solution.py:20
  130.5 0.7 copy-start.5
  136.1 283.9 %collective-permute-start.6 = (bf16[32,640]{1,0:T(8,128)(2,1)S(1)}, bf16[32,640]{1,0:T(8,128)(2,1)S(1)}, u32[]{:S(2)}, u32[]{:S(2)}) collective-permute-start(bf16[32,640]{1,0:T(8,128)(2,1)S(1)} %copy_bitcast_fusion), channel_id=1, source_target_pairs={{0,8},{8,0},{4,12},{12,4},{16,24},{24,16},{20,28},{28,20},{32,40},... | collective-permute-start | bytes 122888 | tf_op jit(solution)/shard_map/ppermute | solution.py:20
  138.7 286.1 %collective-permute-start.4 = (bf16[32,640]{1,0:T(8,128)(2,1)S(1)}, bf16[32,640]{1,0:T(8,128)(2,1)S(1)}, u32[]{:S(2)}, u32[]{:S(2)}) collective-permute-start(bf16[32,640]{1,0:T(8,128)(2,1)S(1)} %copy_bitcast_fusion.1), channel_id=1, source_target_pairs={{0,8},{8,0},{4,12},{12,4},{16,24},{24,16},{20,28},{28,20},{32,40},... | collective-permute-start | bytes 122888 | tf_op jit(solution)/shard_map/ppermute | solution.py:20
  420.0 6.7 %collective-permute-start.7 = (bf16[16,640]{1,0:T(8,128)(2,1)S(1)}, bf16[16,640]{1,0:T(8,128)(2,1)S(1)}, u32[]{:S(2)}, u32[]{:S(2)}) collective-permute-start(bf16[16,640]{1,0:T(8,128)(2,1)S(1)} %select_convert_fusion.2), channel_id=1, source_target_pairs={{0,4},{4,0},{8,12},{12,8},{16,20},{20,16},{24,28},{28,24},{32,36},... | collective-permute-start | bytes 61448 | tf_op jit(solution)/shard_map/ppermute | solution.py:20
  424.8 5.7 %collective-permute-start.5 = (bf16[16,640]{1,0:T(8,128)(2,1)S(1)}, bf16[16,640]{1,0:T(8,128)(2,1)S(1)}, u32[]{:S(2)}, u32[]{:S(2)}) collective-permute-start(bf16[16,640]{1,0:T(8,128)(2,1)S(1)} %select_convert_fusion.3), channel_id=1, source_target_pairs={{0,4},{4,0},{8,12},{12,8},{16,20},{20,16},{24,28},{28,24},{32,36},... | collective-permute-start | bytes 61448 | tf_op jit(solution)/shard_map/ppermute | solution.py:20
  430.6 1.2 copy-start.3
Sparse Core Ops, SparseCore 0:
  144.4 154.0 all-reduce.4
where the time goes:
time: 444 us; the launch traced here: 443 us
  blocking collectives  372 us (84%)
  starting transfers between devices  26.2 us (6%)
  between operations  15.2 us (3%)
  local copies, waits for them, and re-layouts  12.3 us (3%)
  waiting for transfers between devices  7.26 us (2%)
  matrix products  6.13 us (1%)
    psum x1, blocking collectives, shards(): gain_grad = lax.psum(gain_part, ('dp', 'ctx'))  276 us
    all_gather x1, blocking collectives, shards(): lax.all_gather(top_keys, 'ctx', axis=0, tiled=True)  48.5 us
    all_gather x1, blocking collectives, shards(): lax.all_gather(top_vals, 'ctx', axis=0, tiled=True)  47.4 us
    ppermute x8, starting transfers between devices, swapped(): return lax.ppermute(block, axis, route)  26.1 us
  transfers between devices with their start and end apart: 9, of which 3 were waited for; matrix products, arithmetic and copies ran while one was open for 2% of the time, Pallas kernels for 0%

commit v1 on v0

--- a/solution.py
+++ b/solution.py
@@ -146,7 +146,7 @@
     attended = (normed * gain_rows).astype(jnp.bfloat16).reshape(1, tokens, flat_width)
     grad_full = grad_y[0].reshape(row_shape).astype(jnp.float32)
     gain_part = jnp.sum(grad_full * normed, axis=0).reshape(flat_width)
-    gain_grad = lax.psum(gain_part, ("dp", "ctx"))
+    gain_grad = lax.psum(lax.psum(gain_part, "ctx"), "dp")
     grad_norm = grad_full * gain_rows
     grad_attn = inv_rms * (
         grad_norm - normed * jnp.mean(grad_norm * normed, axis=-1, keepdims=True)

time: 444 us -> 317 us (0.71)
  the two profiles are of different devices: /device:TPU:266 before, /device:TPU:2 now
where the time goes in v1:
time: 317 us
  blocking collectives  248 us (78%)
  starting transfers between devices  25.3 us (8%)
  between operations  15.2 us (5%)
  local copies, waits for them, and re-layouts  12.3 us (4%)
  matrix products  6.13 us (2%)
  waiting for transfers between devices  5.29 us (2%)
  other arithmetic  4.4 us (1%)
    psum x2, blocking collectives, shards(): gain_grad = lax.psum(lax.psum(gain_part, 'ctx'), 'dp')  144 us
    all_gather x1, blocking collectives, shards(): lax.all_gather(top_keys, 'ctx', axis=0, tiled=True)  56.5 us
    all_gather x1, blocking collectives, shards(): lax.all_gather(top_vals, 'ctx', axis=0, tiled=True)  47.7 us
    ppermute x8, starting transfers between devices, swapped(): return lax.ppermute(block, axis, route)  25.3 us
    unnamed x25, local copies, waits for them, and re-layouts  8.48 us
  transfers between devices with their start and end apart: 9, of which 4 were waited for; matrix products, arithmetic and copies ran while one was open for 2% of the time, Pallas kernels for 0%

profile of v1, /device:TPU:2, one launch (start us, length us, event | category | flops | bytes accessed | tf_op | source)
XLA Modules:
  0.0 316.6 jit_solution(4417123547839130465)
XLA Ops:
  7.2 0.8 slice_bitcast_fusion.1
  8.0 1.5 fusion.26
  9.6 3.5 %collective-permute-start = (bf16[16,640]{1,0:T(8,128)(2,1)S(1)}, bf16[16,640]{1,0:T(8,128)(2,1)S(1)}, u32[]{:S(2)}, u32[]{:S(2)}) collective-permute-start(bf16[16,640]{1,0:T(8,128)(2,1)S(1)} %copy_bitcast_fusion.7), channel_id=1, source_target_pairs={{0,4},{4,0},{8,12},{12,8},{16,20},{20,16},{24,28},{28,24},{32,36},... | collective-permute-start | bytes 61448 | tf_op jit(solution)/shard_map/ppermute | solution.py:20
  13.1 2.5 collective-permute-start.2
  15.6 0.2 copy.143
  15.8 0.2 copy.144
  15.9 0.2 reshape_reshape_squeeze.20
  16.2 0.2 reshape_reshape_squeeze.21
  16.4 0.7 copy-done.2
  17.1 0.2 reshape_reshape_squeeze.23
  17.5 0.3 select_reduce_fusion
  17.8 56.5 %all-gather = bf16[64,2,640]{2,1,0:T(2,128)(2,1)S(1)} all-gather(bf16[1,2,640]{2,1,0:T(2,128)(2,1)S(1)} %reshape.367), channel_id=1, replica_groups=mesh['dp'=2,'ctx'=64,'head'=4] {'ctx'}, dimensions={0}, use_global_device_ids=true | all-gather | bytes 166400 | tf_op jit(solution)/shard_map/all_gather | solution.py:117
  74.4 0.3 fusion.58
  74.7 0.2 exponential_reduce_fusion.2
  75.0 47.7 %all-gather.1 = bf16[64,2,640]{2,1,0:T(2,128)(2,1)S(1)} all-gather(bf16[1,2,640]{2,1,0:T(2,128)(2,1)S(1)} %reshape.369), channel_id=1, replica_groups=mesh['dp'=2,'ctx'=64,'head'=4] {'ctx'}, dimensions={0}, use_global_device_ids=true | all-gather | bytes 166400 | tf_op jit(solution)/shard_map/all_gather | solution.py:118
  122.8 0.2 convolution_bitcast_fusion.9
  122.9 0.3 fusion.60
  123.3 0.2 copy.157
  123.7 0.5 copy-done.4
  124.2 0.2 copy.168
  124.7 1.3 dynamic-slice
  126.7 2.7 collective-permute-start.1
  129.5 4.0 %collective-permute-start.3 = (bf16[32,640]{1,0:T(8,128)(2,1)S(1)}, bf16[32,640]{1,0:T(8,128)(2,1)S(1)}, u32[]{:S(2)}, u32[]{:S(2)}) collective-permute-start(bf16[32,640]{1,0:T(8,128)(2,1)S(1)} %maximum_select_fusion.4), channel_id=1, source_target_pairs={{0,8},{8,0},{4,12},{12,4},{16,24},{24,16},{20,28},{28,20},{32,40},... | collective-permute-start | bytes 122888 | tf_op jit(solution)/shard_map/ppermute | solution.py:20
  133.5 0.5 collective-permute-done.1
  134.0 0.2 fusion.59
  134.2 0.2 exponential_reduce_fusion.1
  134.8 0.2 fusion.23
  135.1 1.2 collective-permute-done.3
  136.3 0.2 convolution_bitcast_fusion.7
  136.5 0.5 multiply_reduce_fusion.3
  137.0 0.7 copy-done.5
  137.7 0.3 multiply_reduce_fusion
  138.0 0.3 fusion.22
  138.3 0.2 multiply_reduce_fusion.1
  138.6 0.2 fusion.21
  139.2 0.2 fusion.20
  139.4 0.2 convolution_bitcast_fusion.8
  139.5 1.0 fusion.50
  140.5 1.0 fusion.47
  141.5 0.4 fusion.14
  142.0 0.3 convolution_bitcast_fusion.4
  142.4 0.2 fusion.17
  142.6 4.0 %collective-permute-start.6 = (bf16[32,640]{1,0:T(8,128)(2,1)S(1)}, bf16[32,640]{1,0:T(8,128)(2,1)S(1)}, u32[]{:S(2)}, u32[]{:S(2)}) collective-permute-start(bf16[32,640]{1,0:T(8,128)(2,1)S(1)} %copy_bitcast_fusion), channel_id=1, source_target_pairs={{0,8},{8,0},{4,12},{12,4},{16,24},{24,16},{20,28},{28,20},{32,40},... | collective-permute-start | bytes 122888 | tf_op jit(solution)/shard_map/ppermute | solution.py:20
  146.7 0.2 convolution_bitcast_fusion.5
  147.0 2.7 collective-permute-start.4
  149.8 0.2 copy.167
  149.9 0.8 copy.198
  150.8 140.8 %psum.14 = f32[640]{0:T(1024)S(1)} all-reduce(f32[640]{0:T(1024)S(1)} %bitcast.253), channel_id=1, replica_groups=mesh['dp'=2,'ctx'=64,'head'=4] {'ctx'}, use_global_device_ids=true, to_apply=%region_24.25 | all-reduce | flops 640 | bytes 5120 | tf_op jit(solution)/shard_map/psum | solution.py:149
  291.5 3.0 psum.15
  294.6 1.9 collective-permute-start.7
  296.6 3.9 %collective-permute-start.5 = (bf16[16,640]{1,0:T(8,128)(2,1)S(1)}, bf16[16,640]{1,0:T(8,128)(2,1)S(1)}, u32[]{:S(2)}, u32[]{:S(2)}) collective-permute-start(bf16[16,640]{1,0:T(8,128)(2,1)S(1)} %select_convert_fusion.3), channel_id=1, source_target_pairs={{0,4},{4,0},{8,12},{12,8},{16,20},{20,16},{24,28},{28,24},{32,36},... | collective-permute-start | bytes 61448 | tf_op jit(solution)/shard_map/ppermute | solution.py:20
  300.6 1.8 collective-permute-done.5
  302.3 1.8 all-reduce.5.cloned.1.call-done
  304.2 1.2 constant_dynamic-slice_fusion.1
  305.8 0.2 bitcast_select_fusion
  306.0 0.2 fusion.12
  306.2 0.2 copy.187
  306.4 0.8 copy.200
  307.2 0.3 fusion.11
  307.5 0.2 copy.179
  307.7 0.8 copy.199
  308.5 0.3 fusion.13
  308.8 0.2 copy.196
  309.0 0.8 copy.201
  (74 shorter events, 3.0 us)
Async XLA Ops:
  7.2 297.0 %all-reduce.5.cloned.1.call-start = ((), (), s32[]{:S(2)}) async-start(), calls=%async_computation | async-start | bytes 1310720
  8.0 7.6 %copy-start = (bf16[1,128,640]{2,1,0:T(8,128)(2,1)S(1)}, bf16[1,128,640]{2,1,0:T(8,128)(2,1)}, u32[]{:S(2)}) copy-start(bf16[1,128,640]{2,1,0:T(8,128)(2,1)} %param.6) | copy-start | bytes 491524
  9.6 117.0 %collective-permute-start = (bf16[16,640]{1,0:T(8,128)(2,1)S(1)}, bf16[16,640]{1,0:T(8,128)(2,1)S(1)}, u32[]{:S(2)}, u32[]{:S(2)}) collective-permute-start(bf16[16,640]{1,0:T(8,128)(2,1)S(1)} %copy_bitcast_fusion.7), channel_id=1, source_target_pairs={{0,4},{4,0},{8,12},{12,8},{16,20},{20,16},{24,28},{28,24},{32,36},... | collective-permute-start | bytes 61448 | tf_op jit(solution)/shard_map/ppermute | solution.py:20
  13.1 2.7 copy-start.1
  13.1 113.6 %collective-permute-start.2 = (bf16[16,640]{1,0:T(8,128)(2,1)S(1)}, bf16[16,640]{1,0:T(8,128)(2,1)S(1)}, u32[]{:S(2)}, u32[]{:S(2)}) collective-permute-start(bf16[16,640]{1,0:T(8,128)(2,1)S(1)} %copy_bitcast_fusion.6), channel_id=1, source_target_pairs={{0,4},{4,0},{8,12},{12,8},{16,20},{20,16},{24,28},{28,24},{32,36},... | collective-permute-start | bytes 61448 | tf_op jit(solution)/shard_map/ppermute | solution.py:20
  16.2 0.9 copy-start.2
  123.3 0.9 copy-start.4
  126.7 7.2 %collective-permute-start.1 = (bf16[32,640]{1,0:T(8,128)(2,1)S(1)}, bf16[32,640]{1,0:T(8,128)(2,1)S(1)}, u32[]{:S(2)}, u32[]{:S(2)}) collective-permute-start(bf16[32,640]{1,0:T(8,128)(2,1)S(1)} %maximum_select_fusion.2), channel_id=1, source_target_pairs={{0,8},{8,0},{4,12},{12,4},{16,24},{24,16},{20,28},{28,20},{32,40},... | collective-permute-start | bytes 122888 | tf_op jit(solution)/shard_map/ppermute | solution.py:20
  129.5 6.8 %collective-permute-start.3 = (bf16[32,640]{1,0:T(8,128)(2,1)S(1)}, bf16[32,640]{1,0:T(8,128)(2,1)S(1)}, u32[]{:S(2)}, u32[]{:S(2)}) collective-permute-start(bf16[32,640]{1,0:T(8,128)(2,1)S(1)} %maximum_select_fusion.4), channel_id=1, source_target_pairs={{0,8},{8,0},{4,12},{12,4},{16,24},{24,16},{20,28},{28,20},{32,40},... | collective-permute-start | bytes 122888 | tf_op jit(solution)/shard_map/ppermute | solution.py:20
  137.0 0.7 copy-start.5
  142.6 152.0 %collective-permute-start.6 = (bf16[32,640]{1,0:T(8,128)(2,1)S(1)}, bf16[32,640]{1,0:T(8,128)(2,1)S(1)}, u32[]{:S(2)}, u32[]{:S(2)}) collective-permute-start(bf16[32,640]{1,0:T(8,128)(2,1)S(1)} %copy_bitcast_fusion), channel_id=1, source_target_pairs={{0,8},{8,0},{4,12},{12,4},{16,24},{24,16},{20,28},{28,20},{32,40},... | collective-permute-start | bytes 122888 | tf_op jit(solution)/shard_map/ppermute | solution.py:20
  147.0 149.5 %collective-permute-start.4 = (bf16[32,640]{1,0:T(8,128)(2,1)S(1)}, bf16[32,640]{1,0:T(8,128)(2,1)S(1)}, u32[]{:S(2)}, u32[]{:S(2)}) collective-permute-start(bf16[32,640]{1,0:T(8,128)(2,1)S(1)} %copy_bitcast_fusion.1), channel_id=1, source_target_pairs={{0,8},{8,0},{4,12},{12,4},{16,24},{24,16},{20,28},{28,20},{32,40},... | collective-permute-start | bytes 122888 | tf_op jit(solution)/shard_map/ppermute | solution.py:20
  294.6 5.9 %collective-permute-start.7 = (bf16[16,640]{1,0:T(8,128)(2,1)S(1)}, bf16[16,640]{1,0:T(8,128)(2,1)S(1)}, u32[]{:S(2)}, u32[]{:S(2)}) collective-permute-start(bf16[16,640]{1,0:T(8,128)(2,1)S(1)} %select_convert_fusion.2), channel_id=1, source_target_pairs={{0,4},{4,0},{8,12},{12,8},{16,20},{20,16},{24,28},{28,24},{32,36},... | collective-permute-start | bytes 61448 | tf_op jit(solution)/shard_map/ppermute | solution.py:20
  296.6 5.7 %collective-permute-start.5 = (bf16[16,640]{1,0:T(8,128)(2,1)S(1)}, bf16[16,640]{1,0:T(8,128)(2,1)S(1)}, u32[]{:S(2)}, u32[]{:S(2)}) collective-permute-start(bf16[16,640]{1,0:T(8,128)(2,1)S(1)} %select_convert_fusion.3), channel_id=1, source_target_pairs={{0,4},{4,0},{8,12},{12,8},{16,20},{20,16},{24,28},{28,24},{32,36},... | collective-permute-start | bytes 61448 | tf_op jit(solution)/shard_map/ppermute | solution.py:20
  304.2 1.2 copy-start.3
Sparse Core Ops, SparseCore 0:
  150.9 153.2 all-reduce.4
